TPU v7x, 32 devices: a whole 2x2x4 slice. The times are simulated.
32 devices in a mesh: fsdp: 16 (over z, y, core), ctx: 2 (over x).
Axes of the slice: x: 2, y: 2, z: 4, core: 2. Of those that a mesh axis runs over, the one named last changes fastest.
Arguments:
- q_nope: bfloat16 [16, 256, 1024], P('fsdp', 'ctx'), may hold values from -6 to 6
- q_rope: bfloat16 [16, 256, 512], P('fsdp', 'ctx'), may hold values from -450 to 450
- kv_latent: bfloat16 [16, 256, 512], P('fsdp', 'ctx'), may hold values from -6 to 6
- key_rope: bfloat16 [16, 256, 64], P('fsdp', 'ctx'), may hold values from -6 to 6
- weight_codes: bfloat16 [512, 2048], P('fsdp'), may hold values from -0.25 to 0.25
- exponents: int32 [4, 16], replicated, may hold values from -1 to 1
- doc_ids: int32 [16, 256], P('fsdp'), may hold values from 0 to 3, never falling along the last dimension, each value on 1 to 128 neighbouring positions
Outputs:
- scaled_out: bfloat16 [16, 256, 1024], P('fsdp', 'ctx')
Inputs may be any that keep to these rules, and one draw needn't show every extreme that they name: `doc_ids`: each document of a sequence covers consecutive positions, at most 128 of them.
All inputs are finite; a program needn't handle non-finite values. Where the computation divides by a largest or mean magnitude, that divisor is 1e-20 or more.
Results may differ from a plain program's by a relative error of at most 0.0085.
Values may be sent and summed in bfloat16 or wider, within the bound.
A program may use at most 64 MiB of HBM per device.

v0:
```python
import jax
import jax.numpy as jnp
from jax import lax
from jax.sharding import PartitionSpec as P

DN = 128
DR = 64
DV = 128
BLK = 128


def dequantize(codes, exponents):
    nrow, ncol = exponents.shape
    factor = jnp.exp2(exponents.astype(jnp.float32)).astype(jnp.bfloat16)
    scaled = codes.reshape(nrow, BLK, ncol, BLK) * factor[:, None, :, None]
    return scaled.reshape(codes.shape)


def attend(queries, rotary, keys_values, rope_all, query_places, query_docs, docs):
    length = keys_values.shape[0]
    k_nope = keys_values[:, :, :DN]
    values = keys_values[:, :, DN:]
    scores = jnp.einsum("qhd,khd->hqk", queries, k_nope, preferred_element_type=jnp.float32)
    scores = scores + jnp.einsum(
        "qhd,kd->hqk", rotary, rope_all, preferred_element_type=jnp.float32
    )
    scores = scores * (DN + DR) ** (-0.5)
    key_places = jnp.arange(length, dtype=jnp.int32)
    allowed = (key_places[None, :] <= query_places[:, None]) & (
        docs[None, :] == query_docs[:, None]
    )
    scores = jnp.where(allowed[None], scores, jnp.float32(-1e30))
    top = jnp.max(scores, axis=-1, keepdims=True)
    expo = jnp.exp(scores - top)
    probs = (expo / jnp.sum(expo, axis=-1, keepdims=True)).astype(jnp.bfloat16)
    return jnp.einsum("hqk,khd->qhd", probs, values, preferred_element_type=jnp.float32)


def per_device(q_nope, q_rope, kv_latent, key_rope, weight_codes, exponents, doc_ids):
    tok = q_nope.shape[1]
    heads = q_nope.shape[2] // DN
    groups = lax.axis_size("ctx")
    length = tok * groups
    offset = lax.axis_index("ctx") * tok
    docs = doc_ids[0]
    latent_all, rope_all = (
        lax.all_gather(kv_latent[0], "ctx", axis=0, tiled=True),
        lax.all_gather(key_rope[0], "ctx", axis=0, tiled=True),
    )
    codes = lax.all_gather(weight_codes, "fsdp", axis=0, tiled=True)
    weight = dequantize(codes, exponents)
    keys_values = jnp.dot(latent_all, weight, preferred_element_type=jnp.float32).astype(
        jnp.bfloat16
    )
    keys_values = keys_values.reshape(length, heads, DN + DV)
    queries = q_nope[0].reshape(tok, heads, DN)
    rotary = q_rope[0].reshape(tok, heads, DR)
    query_docs = lax.dynamic_slice_in_dim(docs, offset, tok)
    query_places = offset + jnp.arange(tok, dtype=jnp.int32)
    attended = attend(queries, rotary, keys_values, rope_all, query_places, query_docs, docs)
    attended = attended.reshape(tok, heads * DV)
    amax = lax.pmax(jnp.max(jnp.abs(attended)), ("fsdp", "ctx"))
    return (attended / amax).reshape(1, tok, heads * DV).astype(jnp.bfloat16)


def solution(mesh):
    in_specs = (
        P("fsdp", "ctx", None),
        P("fsdp", "ctx", None),
        P("fsdp", "ctx", None),
        P("fsdp", "ctx", None),
        P("fsdp", None),
        P(),
        P("fsdp", None),
    )
    out_specs = P("fsdp", "ctx", None)
    return jax.shard_map(
        per_device, mesh=mesh, in_specs=in_specs, out_specs=out_specs, check_vma=False
    )
```

profile of v0, /device:TPU:0, one launch (start us, length us, event | category | flops | bytes accessed | tf_op | source)
XLA Modules:
  0.0 105.1 jit_solution(8917940227443522955)
XLA Ops:
  6.5 0.0 all-gather.4.cloned.1.call-start
  6.5 0.7 all-gather.4.cloned.1.call-update
  7.3 1.0 copy.21
  8.3 1.0 copy.15
  9.3 5.6 %all-gather.1 = bf16[1,256,64]{1,2,0:T(8,128)(2,1)S(1)} all-gather(bf16[1,128,64]{1,2,0:T(8,128)(2,1)} %param.10), channel_id=3, replica_groups=mesh['fsdp'=16,'ctx'=2] {'ctx'}, dimensions={1}, use_global_device_ids=true | all-gather | bytes 49152 | tf_op jit(solution)/shard_map/all_gather | solution.py:48
  14.9 5.8 %all-gather = bf16[1,256,512]{2,1,0:T(8,128)(2,1)S(1)} all-gather(bf16[1,128,512]{2,1,0:T(8,128)(2,1)} %param.9), channel_id=2, replica_groups=mesh['fsdp'=16,'ctx'=2] {'ctx'}, dimensions={1}, use_global_device_ids=true | all-gather | bytes 393216 | tf_op jit(solution)/shard_map/all_gather | solution.py:47
  20.8 0.7 dynamic-slice_bitcast_fusion
  21.4 0.7 exponential_convert_fusion
  22.1 0.8 fusion.12
  22.9 30.8 %all-gather.4.cloned.1.call-done = bf16[512,2048]{1,0:T(8,128)(2,1)} async-done(((bf16[32,2048]{1,0:T(8,128)(2,1)}), bf16[512,2048]{1,0:T(8,128)(2,1)}) %all-gather.4.cloned.1.call-update) | async-done | bytes 2097168 | tf_op jit(solution)/shard_map/all_gather | solution.py:50
  53.7 0.0 copy-start
  53.7 0.3 mul.20
  54.1 1.2 %copy-done = bf16[512,2048]{1,0:T(8,128)(2,1)S(1)} copy-done((bf16[512,2048]{1,0:T(8,128)(2,1)S(1)}, bf16[512,2048]{1,0:T(8,128)(2,1)}, u32[]{:S(2)}) %copy-start) | copy-done | bytes 2097176
  55.3 1.2 %convolution_convert_fusion = bf16[2048,256]{1,0:T(8,128)(2,1)S(1)} fusion(bf16[512,2048]{1,0:T(8,128)(2,1)S(1)} %copy-done, bf16[64,8,16,128]{3,2,1,0:T(8,128)(2,1)S(1)} %bitcast.38, bf16[1,256,512]{2,1,0:T(8,128)(2,1)S(1)} %all-gather), kind=kOutput, calls=%fused_computation.1 | convolution fusion | flops 538443776 | bytes 5505024 | tf_op jit(solution)/shard_map/dot_general | solution.py:52
  56.5 0.3 convolution_bitcast_fusion.1
  56.9 0.3 fusion.6
  57.2 0.2 fusion.15
  57.5 1.0 abs_reduce_fusion
  58.5 38.2 %pmax.7 = f32[]{:T(128)} all-reduce(f32[]{:T(128)} %get-tuple-element.5), channel_id=1, replica_groups=mesh['fsdp'=16,'ctx'=2] {'fsdp','ctx'}, use_global_device_ids=true, to_apply=%region_3.4 | all-reduce | flops 1 | bytes 8 | tf_op jit(solution)/shard_map/pmax | solution.py:62
  96.7 0.7 divide_convert_fusion.1
  97.4 0.9 copy.17
  (1 shorter events, 0.0 us)
Async XLA Ops:
  6.5 47.2 %all-gather.4.cloned.1.call-start = ((), (), s32[]{:S(2)}) async-start(), calls=%async_computation | async-start | bytes 2228224 | tf_op jit(solution)/shard_map/all_gather | solution.py:50
  53.7 1.6 %copy-start = (bf16[512,2048]{1,0:T(8,128)(2,1)S(1)}, bf16[512,2048]{1,0:T(8,128)(2,1)}, u32[]{:S(2)}) copy-start(bf16[512,2048]{1,0:T(8,128)(2,1)} %all-gather.4.cloned.1.call-done) | copy-start | bytes 6291460
Sparse Core Ops, SparseCore 0:
  9.5 44.1 all-gather.3
where the time goes:
time: 105 us
  blocking collectives  49.7 us (47%)
  waiting for transfers between devices  31.5 us (30%)
  between operations  13.5 us (13%)
  local copies, waits for them, and re-layouts  5.1 us (5%)
  matrix products  2.96 us (3%)
  other arithmetic  2.4 us (2%)
    pmax x1, blocking collectives, per_device(): amax = lax.pmax(jnp.max(jnp.abs(attended)), ('fsdp', 'ctx'))  38.2 us
    all_gather x1, waiting for transfers between devices, per_device(): codes = lax.all_gather(weight_codes, 'fsdp', axis=0, tiled=True)  30.8 us
    all_gather x1, blocking collectives, per_device(): lax.all_gather(kv_latent[0], 'ctx', axis=0, tiled=True)  5.84 us
    all_gather x1, blocking collectives, per_device(): lax.all_gather(key_rope[0], 'ctx', axis=0, tiled=True)  5.64 us
    unnamed x4, local copies, waits for them, and re-layouts  3.26 us
  transfers between devices with their start and end apart: 1, of which 1 were waited for; matrix products, arithmetic and copies ran while one was open for 4% of the time, Pallas kernels for 0%

commit v1 on v0

--- a/solution.py
+++ b/solution.py
@@ -1,6 +1,10 @@
+import functools
+
 import jax
 import jax.numpy as jnp
 from jax import lax
+from jax.experimental import pallas as pl
+from jax.experimental.pallas import tpu as pltpu
 from jax.sharding import PartitionSpec as P
 
 DN = 128
@@ -63,6 +67,300 @@
     return (attended / amax).reshape(1, tok, heads * DV).astype(jnp.bfloat16)
 
 
+MESH = pl.DeviceIdType.MESH
+LANES = 128
+CHUNKS = 2
+
+
+def fused_kernel(
+    n, groups, qn_hbm, qr_hbm, lat_hbm, rope_hbm, codes_hbm, expo_ref, docs_ref,
+    att_ref, amax_ref,
+    weight, lat_all, rope_all, qn, qr, peaks,
+    z_send, z_recv, y_send, y_recv, x_send, x_recv, c_send, c_recv,
+    lat_send, lat_recv, local_sem, own_sem, peak_send, peak_recv, ready,
+):
+    planes = n // 4
+    rows, width = codes_hbm.shape
+    tok = qn_hbm.shape[0]
+    heads = width // (DN + DV)
+    f = lax.axis_index("fsdp")
+    x = lax.axis_index("ctx")
+    core, row, plane = f % 2, (f // 2) % 2, f // 4
+
+    def at(plane_of, row_of, core_of):
+        return (plane_of * 2 + row_of) * 2 + core_of
+
+    to_core = (at(plane, row, 1 - core), x)
+    to_row = (at(plane, 1 - row, core), x)
+    to_ctx = (f, 1 - x)
+    steps = ((1, plane + 1 < planes), (-1, plane >= 1))
+
+    own = pl.ds(pl.multiple_of(x * tok, tok), tok)
+    locals_ = [
+        pltpu.make_async_copy(lat_hbm, lat_all.at[own], local_sem.at[0]),
+        pltpu.make_async_copy(rope_hbm, rope_all.at[own], local_sem.at[1]),
+        pltpu.make_async_copy(qn_hbm, qn, local_sem.at[2]),
+        pltpu.make_async_copy(qr_hbm, qr, local_sem.at[3]),
+        pltpu.make_async_copy(
+            codes_hbm, weight.at[pl.ds(pl.multiple_of(f * rows, rows), rows)], own_sem
+        ),
+    ]
+    for copy in locals_:
+        copy.start()
+
+    barrier = pltpu.get_barrier_semaphore()
+    for target in (to_core, to_row, to_ctx):
+        pl.semaphore_signal(barrier, inc=1, device_id=target, device_id_type=MESH)
+    count = 3
+    for step, there in steps:
+        count = count + there.astype(jnp.int32)
+
+        @pl.when(there)
+        def _(step=step):
+            pl.semaphore_signal(
+                barrier, inc=1, device_id=(at(plane + step, row, core), x), device_id_type=MESH
+            )
+
+    pl.semaphore_wait(barrier, count)
+
+    cut = width // CHUNKS
+    half = cut // 2
+
+    def whole(j):
+        return pl.ds(j * cut, cut)
+
+    def part(j, which):
+        return pl.ds(pl.multiple_of(j * cut + which * half, LANES), half)
+
+    def piece(plane_of, row_of, core_of, columns):
+        start = pl.multiple_of(at(plane_of, row_of, core_of) * rows, rows)
+        return weight.at[pl.ds(start, rows), columns]
+
+    def remote(src, dst, send, recv, target):
+        return pltpu.make_async_remote_copy(
+            src_ref=src, dst_ref=dst, send_sem=send, recv_sem=recv,
+            device_id=target, device_id_type=MESH,
+        )
+
+    def along(k, d, j, step):
+        src = plane - step * k
+        dst = piece(src, row, core, whole(j))
+        origin = codes_hbm.at[:, whole(j)] if k == 0 else dst
+        return remote(
+            origin, dst, z_send.at[k, d, j], z_recv.at[k, d, j], (at(plane + step, row, core), x)
+        )
+
+    def along_in(k, d, j, step):
+        dst = piece(plane - step * k, row, core, whole(j))
+        return remote(dst, dst, z_send.at[k - 1, d, j], z_recv.at[k - 1, d, j], to_core)
+
+    def rowwise(k, d, j, step):
+        dst = piece(plane - step * k, row, core, part(j, x))
+        origin = codes_hbm.at[:, part(j, x)] if k == 0 else dst
+        return remote(origin, dst, y_send.at[k, d, j], y_recv.at[k, d, j], to_row)
+
+    def rowwise_in(k, d, j, step):
+        dst = piece(plane - step * k, 1 - row, core, part(j, x))
+        return remote(dst, dst, y_send.at[k, d, j], y_recv.at[k, d, j], to_row)
+
+    def ctxwise(k, d, j, step):
+        dst = piece(plane - step * k, 1 - row, core, part(j, x))
+        return remote(dst, dst, x_send.at[k, d, j], x_recv.at[k, d, j], to_ctx)
+
+    def ctxwise_in(k, d, j, step):
+        dst = piece(plane - step * k, 1 - row, core, part(j, 1 - x))
+        return remote(dst, dst, x_send.at[k, d, j], x_recv.at[k, d, j], to_ctx)
+
+    def corewise(k, d, j, step, which):
+        src = plane - step * k
+        dst = (
+            piece(src, row, core, whole(j))
+            if which == 0
+            else piece(src, 1 - row, core, part(j, x if which == 1 else 1 - x))
+        )
+        origin = codes_hbm.at[:, whole(j)] if which == 0 and k == 0 else dst
+        return remote(origin, dst, c_send.at[which, k, d, j], c_recv.at[which, k, d, j], to_core)
+
+    def corewise_in(k, d, j, step, which):
+        src = plane - step * k
+        dst = (
+            piece(src, row, 1 - core, whole(j))
+            if which == 0
+            else piece(src, 1 - row, 1 - core, part(j, x if which == 1 else 1 - x))
+        )
+        return remote(dst, dst, c_send.at[which, k, d, j], c_recv.at[which, k, d, j], to_core)
+
+    def each(k, body):
+        for d, (step, there) in enumerate(steps if k else steps[:1]):
+            if k == 0:
+                body(d, step)
+            else:
+                src = plane - step * k
+                pl.when((src >= 0) & (src < planes))(functools.partial(body, d, step))
+
+    def z_stage(k, j):
+        def body(d, step):
+            if k:
+                along_in(k, d, j, step).wait_recv()
+            for e, (onward, there) in enumerate(steps):
+                if k == 0 or e == d:
+                    if k < planes - 1:
+                        pl.when(there)(along(k, e, j, onward).start)
+            rowwise(k, d, j, step).start()
+            corewise(k, d, j, step, 0).start()
+
+        each(k, body)
+
+    def y_stage(k, j):
+        def body(d, step):
+            rowwise_in(k, d, j, step).wait_recv()
+            ctxwise(k, d, j, step).start()
+            corewise(k, d, j, step, 1).start()
+
+        each(k, body)
+
+    def x_stage(k, j):
+        def body(d, step):
+            ctxwise_in(k, d, j, step).wait_recv()
+            corewise(k, d, j, step, 2).start()
+
+        each(k, body)
+
+    lat_copies = [
+        remote(lat_hbm, lat_all.at[own], lat_send.at[0], lat_recv.at[0], to_ctx),
+        remote(rope_hbm, rope_all.at[own], lat_send.at[1], lat_recv.at[1], to_ctx),
+    ]
+    order = [(k, j) for k in range(planes) for j in range(CHUNKS)]
+    for t in range(len(order) + 2):
+        if t < len(order):
+            z_stage(*order[t])
+        if t == 0:
+            for copy in lat_copies:
+                copy.start()
+        if 0 <= t - 1 < len(order):
+            y_stage(*order[t - 1])
+        if 0 <= t - 2:
+            x_stage(*order[t - 2])
+    for copy in locals_:
+        copy.wait()
+    for copy in lat_copies:
+        copy.wait()
+    for k, j in order:
+        for which in range(3):
+            each(k, lambda d, step: corewise_in(k, d, j, step, which).wait_recv())
+
+    pl.semaphore_signal(ready, inc=1, device_id=to_ctx, device_id_type=MESH)
+
+    length = lat_all.shape[0]
+    docs = docs_ref[...].astype(jnp.float32)
+    mine = docs_ref[:, own].astype(jnp.float32)
+    mine = jnp.broadcast_to(mine, (tok, tok)).T[:, :1]
+    places = lax.broadcasted_iota(jnp.int32, (tok, length), 0) + x * tok
+    keys_at = lax.broadcasted_iota(jnp.int32, (tok, length), 1)
+    allowed = (keys_at <= places) & (jnp.broadcast_to(docs, (tok, length)) == mine)
+    latents = lat_all[...]
+    rope = rope_all[...]
+    blank = jnp.zeros_like(rope)
+    rope_of = (
+        jnp.concatenate([rope, blank], axis=1), jnp.concatenate([blank, rope], axis=1)
+    )
+    dims_t = (((1,), (1,)), ((), ()))
+    peak = jnp.zeros((tok, DV), jnp.float32)
+    for h in range(heads):
+        at_col = h * (DN + DV)
+        blocks = []
+        for b in range(weight.shape[0] // BLK):
+            line = []
+            for c in range((DN + DV) // BLK):
+                power = jnp.full((1, BLK), expo_ref[b, at_col // BLK + c], jnp.int32)
+                factor = jnp.exp2(power.astype(jnp.float32)).astype(jnp.bfloat16)
+                line.append(
+                    weight[b * BLK : (b + 1) * BLK, at_col + c * BLK : at_col + (c + 1) * BLK]
+                    * factor
+                )
+            blocks.append(jnp.concatenate(line, axis=1))
+        scaled = jnp.concatenate(blocks, axis=0)
+        kv = jnp.dot(latents, scaled, preferred_element_type=jnp.float32).astype(jnp.bfloat16)
+        pair = (h // 2) * 2 * DR
+        queries = jnp.concatenate(
+            [qn[:, h * DN : (h + 1) * DN], qr[:, pair : pair + 2 * DR]], axis=1
+        )
+        keys = jnp.concatenate([kv[:, :DN], rope_of[h % 2]], axis=1)
+        scores = lax.dot_general(queries, keys, dims_t, preferred_element_type=jnp.float32)
+        scores = jnp.where(allowed, scores * (DN + DR) ** (-0.5), jnp.float32(-1e30))
+        top = jnp.max(scores, axis=-1, keepdims=True)
+        expo = jnp.exp(scores - top)
+        total = jnp.sum(expo, axis=-1, keepdims=True)
+        out = jnp.dot(
+            expo.astype(jnp.bfloat16), kv[:, DN:], preferred_element_type=jnp.float32
+        ) / total
+        att_ref[:, h * DV : (h + 1) * DV] = out
+        peak = jnp.maximum(peak, jnp.abs(out))
+
+    me = f * groups + x
+    peaks[me] = jnp.max(peak, axis=0, keepdims=True)
+    pl.semaphore_wait(ready, 1)
+    everyone = n * groups
+    for i in range(1, everyone):
+        other = lax.rem(me + i, everyone)
+        remote(
+            peaks.at[me], peaks.at[me], peak_send, peak_recv, (other // groups, other % groups)
+        ).start()
+    for copy_k, j in order:
+        for e, (onward, there) in enumerate(steps):
+            if copy_k < planes - 1:
+                src = plane - onward * copy_k
+                pl.when(there & (src >= 0) & (src < planes))(
+                    along(copy_k, e, j, onward).wait_send
+                )
+
+        def sent(d, step, k=copy_k, j=j):
+            rowwise(k, d, j, step).wait_send()
+            ctxwise(k, d, j, step).wait_send()
+            for which in range(3):
+                corewise(k, d, j, step, which).wait_send()
+
+        each(copy_k, sent)
+    others = peaks.at[pl.ds(0, everyone - 1)]
+    arrived = remote(others, others, peak_send, peak_recv, to_ctx)
+    arrived.wait_send()
+    arrived.wait_recv()
+    amax_ref[...] = jnp.full(amax_ref.shape, jnp.max(peaks[...]), jnp.float32)
+
+
+def fused(n, groups, q_nope, q_rope, kv_latent, key_rope, weight_codes, exponents, doc_ids):
+    tok = q_nope.shape[1]
+    rows, width = weight_codes.shape
+    planes = n // 4
+    hbm = pl.BlockSpec(memory_space=pl.ANY)
+    vmem = pl.BlockSpec(memory_space=pltpu.VMEM)
+    dma = pltpu.SemaphoreType.DMA
+    links = (planes, 2, CHUNKS)
+    attended, amax = pl.pallas_call(
+        functools.partial(fused_kernel, n, groups),
+        out_shape=(
+            jax.ShapeDtypeStruct((tok, width // 2), jnp.float32),
+            jax.ShapeDtypeStruct((1, LANES), jnp.float32),
+        ),
+        in_specs=[hbm] * 5 + [pl.BlockSpec(memory_space=pltpu.SMEM), vmem],
+        out_specs=(vmem, vmem),
+        scratch_shapes=[
+            pltpu.VMEM((rows * n, width), jnp.bfloat16),
+            pltpu.VMEM((tok * groups, kv_latent.shape[2]), jnp.bfloat16),
+            pltpu.VMEM((tok * groups, key_rope.shape[2]), jnp.bfloat16),
+            pltpu.VMEM(q_nope.shape[1:], jnp.bfloat16),
+            pltpu.VMEM(q_rope.shape[1:], jnp.bfloat16),
+            pltpu.VMEM((n * groups, 1, LANES), jnp.float32),
+            dma(links), dma(links), dma(links), dma(links), dma(links), dma(links),
+            dma((3, *links)), dma((3, *links)),
+            dma((2,)), dma((2,)), dma((4,)), dma, dma, dma,
+            pltpu.SemaphoreType.REGULAR,
+        ],
+        compiler_params=pltpu.CompilerParams(collective_id=0, has_side_effects=True),
+    )(q_nope[0], q_rope[0], kv_latent[0], key_rope[0], weight_codes, exponents, doc_ids)
+    return (attended / amax[0, 0]).astype(jnp.bfloat16)[None]
+
+
 def solution(mesh):
     in_specs = (
         P("fsdp", "ctx", None),
@@ -74,6 +372,14 @@
         P("fsdp", None),
     )
     out_specs = P("fsdp", "ctx", None)
+    n, groups = mesh.shape["fsdp"], mesh.shape["ctx"]
+
+    def body(*args):
+        rows = args[4].shape[0]
+        if groups == 2 and n % 4 == 0 and rows % 16 == 0:
+            return fused(n, groups, *args)
+        return per_device(*args)
+
     return jax.shard_map(
-        per_device, mesh=mesh, in_specs=in_specs, out_specs=out_specs, check_vma=False
-    )
+        body, mesh=mesh, in_specs=in_specs, out_specs=out_specs, check_vma=False
+    )

time: 105 us -> 41.3 us (0.39)
  blocking collectives: 49.7 us -> 0 us
  Pallas kernels: 0 us -> 37.1 us
  waiting for transfers between devices: 31.5 us -> 0 us
  between operations: 13.5 us -> 0.02 us
  local copies, waits for them, and re-layouts: 5.1 us -> 2.1 us
  matrix products: 2.96 us -> 0 us
    pmax x1 -> x0, blocking collectives: 38.2 us -> none  [per_device(): amax = lax.pmax(jnp.max(jnp.abs(attended)), ('fsdp', 'ctx'))]
    pallas_call x0 -> x1, Pallas kernels: none -> 37.1 us  [fused(): pl.pallas_call(functools.partial(fused_kernel, n, groups), out_shape=(jax...]
    all_gather x1 -> x0, waiting for transfers between devices: 30.8 us -> none  [per_device(): codes = lax.all_gather(weight_codes, 'fsdp', axis=0, tiled=True)]
    all_gather x2 -> x0, blocking collectives: 11.5 us -> none  [the longest x1 5.84 us: per_device(): lax.all_gather(kv_latent[0], 'ctx', axis=0, tiled=True)]
    dot_general x4 -> x0, matrix products: 2.96 us -> none  [the longest x1 1.23 us: per_device(): jnp.dot(latent_all, weight, preferred_element_type=jnp.float32)]
    broadcast_in_dim x0 -> x1, other arithmetic: none -> 1.82 us  [fused(): return (attended / amax[0, 0]).astype(jnp.bfloat16)[None]]
    convert_element_type x2 -> x0, other arithmetic: 1.38 us -> none  [the longest x1 0.69 us: per_device(): return (attended / amax).reshape(1, tok, heads * DV).astype(jnp.bfloat16)]
    unnamed x4 -> x3, local copies, waits for them, and re-layouts: 3.26 us -> 2.1 us
  transfers between devices with their start and end apart: 1 -> 0, of which waited for: 1 -> 0; matrix products, arithmetic and copies ran while one was open for 4% -> 0% of each run, Pallas kernels for 0% -> 0%
where the time goes in v1:
time: 41.3 us; the launch traced here: 41 us
  Pallas kernels  37.1 us (90%)
  local copies, waits for them, and re-layouts  2.1 us (5%)
  other arithmetic  1.82 us (4%)
    pallas_call x1, Pallas kernels, fused(): pl.pallas_call(functools.partial(fused_kernel, n, groups), out_shape=(jax...  37.1 us
    unnamed x3, local copies, waits for them, and re-layouts  2.1 us
    broadcast_in_dim x1, other arithmetic, fused(): return (attended / amax[0, 0]).astype(jnp.bfloat16)[None]  1.82 us

profile of v1, /device:TPU:0, one launch (start us, length us, event | category | flops | bytes accessed | tf_op | source)
XLA Modules:
  0.0 41.0 jit_solution(5723883678129578596)
XLA Ops:
  0.0 1.4 %copy.8 = bf16[1,128,64]{2,1,0:T(8,128)(2,1)} copy(bf16[1,128,64]{1,2,0:T(8,128)(2,1)} %param.10) | data formatting | bytes 32768 | tf_op args[3]
  1.4 37.1 %shard_map.73 = (f32[128,1024]{1,0:T(8,128)}, f32[1,128]{1,0:T(1,128)}) custom-call(bf16[128,1024]{1,0:T(8,128)(2,1)} %bitcast.8, bf16[128,512]{1,0:T(8,128)(2,1)} %bitcast.9, bf16[128,512]{1,0:T(8,128)(2,1)} %bitcast.10, bf16[128,64]{1,0:T(8,128)(2,1)} %bitcast.11, bf16[32,2048]{1,0:T(8,128)(2,1)} %codes_hbm.1, s32[4,16]{1,0:T(4,128)} %expo_ref.1, ...), custom_call_target="tpu_custom_call" | custom-call | tf_op jit(solution)/shard_map/pallas_call | solution.py:339
  38.5 0.0 copy-start
  38.5 0.7 %copy-done = f32[1,128]{1,0:T(1,128)S(1)} copy-done((f32[1,128]{1,0:T(1,128)S(1)}, f32[1,128]{1,0:T(1,128)}, u32[]{:S(2)}) %copy-start) | copy-done | bytes 536
  39.2 1.8 %fusion = bf16[1,128,1024]{2,1,0:T(8,128)(2,1)} fusion(f32[128,1024]{1,0:T(8,128)} %get-tuple-element.7, f32[]{:T(128)S(1)} %bitcast.12), kind=kLoop, calls=%fused_computation.1 | loop fusion | flops 262144 | bytes 786436 | tf_op jit(solution)/shard_map/broadcast_in_dim | solution.py:361
Async XLA Ops:
  38.5 0.7 %copy-start = (f32[1,128]{1,0:T(1,128)S(1)}, f32[1,128]{1,0:T(1,128)}, u32[]{:S(2)}) copy-start(f32[1,128]{1,0:T(1,128)} %get-tuple-element.8) | copy-start | bytes 1540

commit v2 on v0

--- a/solution.py
+++ b/solution.py
@@ -1,6 +1,10 @@
+import functools
+
 import jax
 import jax.numpy as jnp
 from jax import lax
+from jax.experimental import pallas as pl
+from jax.experimental.pallas import tpu as pltpu
 from jax.sharding import PartitionSpec as P
 
 DN = 128
@@ -63,6 +67,345 @@
     return (attended / amax).reshape(1, tok, heads * DV).astype(jnp.bfloat16)
 
 
+MESH = pl.DeviceIdType.MESH
+LANES = 128
+RELAYED = 2
+
+
+def fused_kernel(
+    n, groups, qn_hbm, qr_hbm, lat_hbm, rope_hbm, codes_hbm, expo_ref, docs_ref,
+    out_ref,
+    weight, lat_all, rope_all, qn, qr, attended, bias, peaks,
+    z_send, z_recv, y_send, y_recv, x_send, x_recv, c_send, c_recv,
+    lat_send, lat_recv, local_sem, own_sem, peak_send, peak_recv, ready, entered,
+):
+    planes = n // 4
+    rows, width = codes_hbm.shape
+    hr = rows // 2
+    tok = qn_hbm.shape[0]
+    heads = width // (DN + DV)
+    f = lax.axis_index("fsdp")
+    x = lax.axis_index("ctx")
+    core, row, plane = f % 2, (f // 2) % 2, f // 4
+
+    def at(plane_of, row_of, core_of):
+        return (plane_of * 2 + row_of) * 2 + core_of
+
+    def inside(p):
+        return (p >= 0) & (p < planes)
+
+    to_core = (at(plane, row, 1 - core), x)
+    to_row = (at(plane, 1 - row, core), x)
+    to_ctx = (f, 1 - x)
+    steps = (1, -1)
+
+    own = pl.ds(pl.multiple_of(x * tok, tok), tok)
+    locals_ = [
+        pltpu.make_async_copy(lat_hbm, lat_all.at[own], local_sem.at[0]),
+        pltpu.make_async_copy(rope_hbm, rope_all.at[:, own], local_sem.at[1]),
+        pltpu.make_async_copy(qn_hbm, qn, local_sem.at[2]),
+        pltpu.make_async_copy(qr_hbm, qr, local_sem.at[3]),
+        pltpu.make_async_copy(
+            codes_hbm, weight.at[pl.ds(pl.multiple_of(f * rows, rows), rows)], own_sem
+        ),
+    ]
+
+    barrier = pltpu.get_barrier_semaphore()
+    for target in (to_core, to_row, to_ctx):
+        pl.semaphore_signal(barrier, inc=1, device_id=target, device_id_type=MESH)
+    count = 3
+    for step in steps:
+        there = inside(plane + step)
+        count = count + there.astype(jnp.int32)
+
+        @pl.when(there)
+        def _(step=step):
+            pl.semaphore_signal(
+                barrier, inc=1, device_id=(at(plane + step, row, core), x), device_id_type=MESH
+            )
+
+    for copy in locals_:
+        copy.start()
+    pl.semaphore_wait(barrier, count)
+
+    def piece(plane_of, row_of, core_of, which):
+        start = pl.multiple_of(at(plane_of, row_of, core_of) * rows + which * hr, hr)
+        return weight.at[pl.ds(start, hr)]
+
+    def own_piece(which):
+        return codes_hbm.at[pl.ds(pl.multiple_of(which * hr, hr), hr)]
+
+    def remote(src, dst, send, recv, target):
+        return pltpu.make_async_remote_copy(
+            src_ref=src, dst_ref=dst, send_sem=send, recv_sem=recv,
+            device_id=target, device_id_type=MESH,
+        )
+
+    def named(c):
+        return x if c == 0 else 1 - x
+
+    def z_out(k, d, c):
+        step = steps[d]
+        source = plane - step if k == RELAYED else plane
+        target = plane + step if k <= RELAYED else plane + step * k
+        dst = piece(source, row, core, named(c))
+        origin = dst if k == RELAYED else own_piece(named(c))
+        copy = remote(
+            origin, dst, z_send.at[k, d, c], z_recv.at[k, d, c], (at(target, row, core), x)
+        )
+        return copy, inside(source) & inside(target)
+
+    def z_in(k, d, c):
+        dst = piece(plane - steps[d] * k, row, core, named(c))
+        return remote(dst, dst, z_send.at[k, d, c], z_recv.at[k, d, c], to_core)
+
+    def y_out(k, d):
+        dst = piece(plane - steps[d] * k, row, core, x)
+        origin = dst if k else own_piece(x)
+        return remote(origin, dst, y_send.at[k, d], y_recv.at[k, d], to_row)
+
+    def y_in(k, d):
+        dst = piece(plane - steps[d] * k, 1 - row, core, x)
+        return remote(dst, dst, y_send.at[k, d], y_recv.at[k, d], to_row)
+
+    def x_out(k, d):
+        dst = piece(plane - steps[d] * k, 1 - row, core, x)
+        return remote(dst, dst, x_send.at[k, d], x_recv.at[k, d], to_ctx)
+
+    def x_in(k, d):
+        dst = piece(plane - steps[d] * k, 1 - row, core, 1 - x)
+        return remote(dst, dst, x_send.at[k, d], x_recv.at[k, d], to_ctx)
+
+    def core_piece(k, d, which, core_of):
+        return piece(
+            plane - steps[d] * k, row if which < 2 else 1 - row, core_of, named(which % 2)
+        )
+
+    def core_out(k, d, which):
+        dst = core_piece(k, d, which, core)
+        origin = own_piece(named(which)) if which < 2 and k == 0 else dst
+        return remote(origin, dst, c_send.at[which, k, d], c_recv.at[which, k, d], to_core)
+
+    def core_in(k, d, which):
+        dst = core_piece(k, d, which, 1 - core)
+        return remote(dst, dst, c_send.at[which, k, d], c_recv.at[which, k, d], to_core)
+
+    def each(k, body):
+        if k == 0:
+            body(0)
+        elif k < planes:
+            for d, step in enumerate(steps):
+                pl.when(inside(plane - step * k))(functools.partial(body, d))
+
+    def z_stage(k, c):
+        def body(d):
+            z_in(k, d, c).wait_recv()
+            if k + 1 == RELAYED:
+                onward, there = z_out(RELAYED, d, c)
+                pl.when(there)(onward.start)
+            if c == 0:
+                y_out(k, d).start()
+            core_out(k, d, c).start()
+
+        each(k, body)
+
+    def y_stage(k):
+        def body(d):
+            y_in(k, d).wait_recv()
+            x_out(k, d).start()
+            core_out(k, d, 2).start()
+
+        each(k, body)
+
+    def x_stage(k):
+        def body(d):
+            x_in(k, d).wait_recv()
+            core_out(k, d, 3).start()
+
+        each(k, body)
+
+    lat_copies = [
+        remote(lat_hbm, lat_all.at[own], lat_send.at[0], lat_recv.at[0], to_ctx),
+        remote(rope_hbm, rope_all.at[:, own], lat_send.at[1], lat_recv.at[1], to_ctx),
+    ]
+    from_source = [k for k in range(1, planes) if k != RELAYED]
+
+    def send_own(k, c):
+        for d in range(2):
+            copy, there = z_out(k, d, c)
+            pl.when(there)(copy.start)
+
+    y_out(0, 0).start()
+    send_own(1, 0)
+    for copy in lat_copies:
+        copy.start()
+    for c in range(2):
+        core_out(0, 0, c).start()
+    for r in range(1, planes - 1):
+        for d, step in enumerate(steps):
+
+            @pl.when(inside(plane + step) & inside(plane - step * r))
+            def _(r=r, d=d, step=step):
+                pl.semaphore_signal(
+                    entered.at[r, d], inc=1,
+                    device_id=(at(plane + step, row, core), x), device_id_type=MESH,
+                )
+
+        for d, step in enumerate(steps):
+
+            @pl.when(inside(plane - step * (r + 1)))
+            def _(r=r, d=d):
+                pl.semaphore_wait(entered.at[r, d], 1)
+
+    for k in from_source[1:]:
+        send_own(k, 0)
+    for k in from_source:
+        send_own(k, 1)
+
+    z_stage(1, 0)
+    y_stage(0)
+    z_stage(1, 1)
+    for k in range(2, planes):
+        z_stage(k, 0)
+    x_stage(0)
+    y_stage(1)
+
+    for copy in locals_:
+        copy.wait()
+    for copy in lat_copies:
+        copy.wait()
+    length = lat_all.shape[0]
+    docs = docs_ref[...].astype(jnp.float32)
+    mine = docs_ref[:, own].astype(jnp.float32)
+    mine = jnp.broadcast_to(mine, (tok, tok)).T[:, :1]
+    places = lax.broadcasted_iota(jnp.int32, (tok, length), 0) + x * tok
+    keys_at = lax.broadcasted_iota(jnp.int32, (tok, length), 1)
+    allowed = (keys_at <= places) & (jnp.broadcast_to(docs, (tok, length)) == mine)
+    bias[...] = jnp.where(allowed, jnp.float32(0), jnp.float32(-1e30))
+
+    for k in range(2, planes):
+        y_stage(k)
+    x_stage(1)
+    for k in range(2, planes):
+        z_stage(k, 1)
+    for k in range(2, planes):
+        x_stage(k)
+    for which in range(4):
+        for k in range(planes):
+            each(k, lambda d: core_in(k, d, which).wait_recv())
+
+    pl.semaphore_signal(ready, inc=1, device_id=to_ctx, device_id_type=MESH)
+
+    latents = lat_all[...]
+    rope = rope_all[...]
+    blank = jnp.zeros_like(rope)
+    rope_of = (
+        jnp.concatenate([rope, blank], axis=0).T, jnp.concatenate([blank, rope], axis=0).T
+    )
+    dims_t = (((1,), (1,)), ((), ()))
+    peak = jnp.zeros((tok, DV), jnp.float32)
+    for h in range(heads):
+        at_col = h * (DN + DV)
+        blocks = []
+        for b in range(weight.shape[0] // BLK):
+            line = []
+            for c in range((DN + DV) // BLK):
+                power = jnp.full((1, BLK), expo_ref[b, at_col // BLK + c], jnp.int32)
+                factor = jnp.exp2(power.astype(jnp.float32)).astype(jnp.bfloat16)
+                line.append(
+                    weight[b * BLK : (b + 1) * BLK, at_col + c * BLK : at_col + (c + 1) * BLK]
+                    * factor
+                )
+            blocks.append(jnp.concatenate(line, axis=1))
+        scaled = jnp.concatenate(blocks, axis=0)
+        kv = jnp.dot(latents, scaled, preferred_element_type=jnp.float32).astype(jnp.bfloat16)
+        pair = (h // 2) * 2 * DR
+        queries = jnp.concatenate(
+            [qn[:, h * DN : (h + 1) * DN], qr[:, pair : pair + 2 * DR]], axis=1
+        )
+        keys = jnp.concatenate([kv[:, :DN], rope_of[h % 2]], axis=1)
+        scores = lax.dot_general(queries, keys, dims_t, preferred_element_type=jnp.float32)
+        scores = scores * (DN + DR) ** (-0.5) + bias[...]
+        top = jnp.max(scores, axis=-1, keepdims=True)
+        expo = jnp.exp(scores - top)
+        total = jnp.sum(expo, axis=-1, keepdims=True)
+        out = jnp.dot(
+            expo.astype(jnp.bfloat16), kv[:, DN:], preferred_element_type=jnp.float32
+        ) / total
+        attended[:, h * DV : (h + 1) * DV] = out
+        peak = jnp.maximum(peak, jnp.abs(out))
+
+    me = f * groups + x
+    peaks[me] = jnp.max(peak, axis=0, keepdims=True)
+    pl.semaphore_wait(ready, 1)
+    everyone = n * groups
+
+    def peak_to(target):
+        remote(peaks.at[me], peaks.at[me], peak_send, peak_recv, target).start()
+
+    for i in range(planes):
+        other = lax.rem(2 * planes - 1 - plane - i, planes)
+        for pair in range(7, 0, -1):
+            ctx_of = x if pair // 4 == 0 else 1 - x
+            row_of = row if pair // 2 % 2 == 0 else 1 - row
+            core_of = core if pair % 2 == 0 else 1 - core
+            peak_to((at(other, row_of, core_of), ctx_of))
+        pl.when(other != plane)(functools.partial(peak_to, (at(other, row, core), x)))
+    for c in range(2):
+        for k in range(1, planes):
+            for d in range(2):
+                copy, there = z_out(k, d, c)
+                pl.when(there)(copy.wait_send)
+
+    def sent(k, d):
+        y_out(k, d).wait_send()
+        x_out(k, d).wait_send()
+        for which in range(4):
+            core_out(k, d, which).wait_send()
+
+    for k in range(planes):
+        each(k, functools.partial(sent, k))
+    others = peaks.at[pl.ds(0, everyone - 1)]
+    arrived = remote(others, others, peak_send, peak_recv, to_ctx)
+    arrived.wait_send()
+    arrived.wait_recv()
+    amax = jnp.max(jnp.max(peaks[...], axis=0), axis=-1, keepdims=True)
+    out_ref[...] = (attended[...] / amax).astype(out_ref.dtype)
+
+
+def fused(n, groups, q_nope, q_rope, kv_latent, key_rope, weight_codes, exponents, doc_ids):
+    tok = q_nope.shape[1]
+    rows, width = weight_codes.shape
+    planes = n // 4
+    hbm = pl.BlockSpec(memory_space=pl.ANY)
+    vmem = pl.BlockSpec(memory_space=pltpu.VMEM)
+    dma = pltpu.SemaphoreType.DMA
+    rope = jnp.swapaxes(key_rope, 1, 2)[0]
+    scaled_out = pl.pallas_call(
+        functools.partial(fused_kernel, n, groups),
+        out_shape=jax.ShapeDtypeStruct((tok, width // 2), jnp.bfloat16),
+        in_specs=[hbm] * 5 + [pl.BlockSpec(memory_space=pltpu.SMEM), vmem],
+        out_specs=vmem,
+        scratch_shapes=[
+            pltpu.VMEM((rows * n, width), jnp.bfloat16),
+            pltpu.VMEM((tok * groups, kv_latent.shape[2]), jnp.bfloat16),
+            pltpu.VMEM((rope.shape[0], tok * groups), jnp.bfloat16),
+            pltpu.VMEM(q_nope.shape[1:], jnp.bfloat16),
+            pltpu.VMEM(q_rope.shape[1:], jnp.bfloat16),
+            pltpu.VMEM((tok, width // 2), jnp.float32),
+            pltpu.VMEM((tok, tok * groups), jnp.float32),
+            pltpu.VMEM((n * groups, 1, LANES), jnp.float32),
+            dma((planes, 2, 2)), dma((planes, 2, 2)),
+            dma((planes, 2)), dma((planes, 2)), dma((planes, 2)), dma((planes, 2)),
+            dma((4, planes, 2)), dma((4, planes, 2)),
+            dma((2,)), dma((2,)), dma((4,)), dma, dma, dma,
+            pltpu.SemaphoreType.REGULAR, pltpu.SemaphoreType.REGULAR((planes, 2)),
+        ],
+        compiler_params=pltpu.CompilerParams(collective_id=0, has_side_effects=True),
+    )(q_nope[0], q_rope[0], kv_latent[0], rope, weight_codes, exponents, doc_ids)
+    return scaled_out[None]
+
+
 def solution(mesh):
     in_specs = (
         P("fsdp", "ctx", None),
@@ -74,6 +417,14 @@
         P("fsdp", None),
     )
     out_specs = P("fsdp", "ctx", None)
+    n, groups = mesh.shape["fsdp"], mesh.shape["ctx"]
+
+    def body(*args):
+        rows = args[4].shape[0]
+        if groups == 2 and n % 4 == 0 and rows % 32 == 0:
+            return fused(n, groups, *args)
+        return per_device(*args)
+
     return jax.shard_map(
-        per_device, mesh=mesh, in_specs=in_specs, out_specs=out_specs, check_vma=False
-    )
+        body, mesh=mesh, in_specs=in_specs, out_specs=out_specs, check_vma=False
+    )

time: 105 us -> 34.7 us (0.33)
  blocking collectives: 49.7 us -> 0 us
  Pallas kernels: 0 us -> 32.8 us
  waiting for transfers between devices: 31.5 us -> 0 us
  between operations: 13.5 us -> 0.01 us
  local copies, waits for them, and re-layouts: 5.1 us -> 1.67 us
  matrix products: 2.96 us -> 0 us
  other arithmetic: 2.4 us -> 0 us
    pmax x1 -> x0, blocking collectives: 38.2 us -> none  [per_device(): amax = lax.pmax(jnp.max(jnp.abs(attended)), ('fsdp', 'ctx'))]
    pallas_call x0 -> x1, Pallas kernels: none -> 32.8 us  [fused(): pl.pallas_call(functools.partial(fused_kernel, n, groups), out_shape=jax....]
    all_gather x1 -> x0, waiting for transfers between devices: 30.8 us -> none  [per_device(): codes = lax.all_gather(weight_codes, 'fsdp', axis=0, tiled=True)]
    all_gather x2 -> x0, blocking collectives: 11.5 us -> none  [the longest x1 5.84 us: per_device(): lax.all_gather(kv_latent[0], 'ctx', axis=0, tiled=True)]
    dot_general x4 -> x0, matrix products: 2.96 us -> none  [the longest x1 1.23 us: per_device(): jnp.dot(latent_all, weight, preferred_element_type=jnp.float32)]
    unnamed x4 -> x1, local copies, waits for them, and re-layouts: 3.26 us -> 1.67 us
    convert_element_type x2 -> x0, other arithmetic: 1.38 us -> none  [the longest x1 0.69 us: per_device(): return (attended / amax).reshape(1, tok, heads * DV).astype(jnp.bfloat16)]
  transfers between devices with their start and end apart: 1 -> 0, of which waited for: 1 -> 0; matrix products, arithmetic and copies ran while one was open for 4% -> 0% of each run, Pallas kernels for 0% -> 0%
where the time goes in v2:
time: 34.7 us; the launch traced here: 34.5 us
  Pallas kernels  32.8 us (95%)
  local copies, waits for them, and re-layouts  1.67 us (5%)
    pallas_call x1, Pallas kernels, fused(): pl.pallas_call(functools.partial(fused_kernel, n, groups), out_shape=jax....  32.8 us
    unnamed x1, local copies, waits for them, and re-layouts  1.67 us

profile of v2, /device:TPU:0, one launch (start us, length us, event | category | flops | bytes accessed | tf_op | source)
XLA Modules:
  0.0 34.5 jit_solution(5325345647237145852)
XLA Ops:
  0.0 32.8 %shard_map.73 = bf16[128,1024]{1,0:T(8,128)(2,1)} custom-call(bf16[128,1024]{1,0:T(8,128)(2,1)} %bitcast.8, bf16[128,512]{1,0:T(8,128)(2,1)} %bitcast.9, bf16[128,512]{1,0:T(8,128)(2,1)} %bitcast.10, bf16[64,128]{1,0:T(8,128)(2,1)} %bitcast.11, bf16[32,2048]{1,0:T(8,128)(2,1)} %codes_hbm.1, s32[4,16]{1,0:T(4,128)} %expo_ref.1, s32[1,256]{1,0:T(1,128)} %docs_ref.1), custom_call_target="tpu_custom_call" | custom-call | tf_op jit(solution)/shard_map/pallas_call | solution.py:384
  32.9 1.7 %copy.9 = bf16[1,128,1024]{2,1,0:T(8,128)(2,1)} copy(bf16[1,128,1024]{2,1,0:T(8,128)(2,1)} %bitcast.7) | data formatting | bytes 524288

commit v3 on v2

--- a/solution.py
+++ b/solution.py
@@ -259,16 +259,16 @@
 
     for k in from_source[1:]:
         send_own(k, 0)
+
+    z_stage(1, 0)
     for k in from_source:
         send_own(k, 1)
-
-    z_stage(1, 0)
     y_stage(0)
-    z_stage(1, 1)
     for k in range(2, planes):
         z_stage(k, 0)
+    y_stage(1)
+    z_stage(1, 1)
     x_stage(0)
-    y_stage(1)
 
     for copy in locals_:
         copy.wait()
@@ -383,7 +383,7 @@
     rope = jnp.swapaxes(key_rope, 1, 2)[0]
     scaled_out = pl.pallas_call(
         functools.partial(fused_kernel, n, groups),
-        out_shape=jax.ShapeDtypeStruct((tok, width // 2), jnp.bfloat16),
+        out_shape=pltpu.VMEM((tok, width // 2), jnp.bfloat16),
         in_specs=[hbm] * 5 + [pl.BlockSpec(memory_space=pltpu.SMEM), vmem],
         out_specs=vmem,
         scratch_shapes=[

time: 34.7 us -> 32.1 us (0.925)
  Pallas kernels: 32.8 us -> 31.2 us
  local copies, waits for them, and re-layouts: 1.67 us -> 0.71 us
    pallas_call x1, Pallas kernels: 32.8 us -> 31.2 us  [fused(): pl.pallas_call(functools.partial(fused_kernel, n, groups), out_shape=pltp...]
    unnamed x1, local copies, waits for them, and re-layouts: 1.67 us -> 0.71 us
where the time goes in v3:
time: 32.1 us; the launch traced here: 31.9 us
  Pallas kernels  31.2 us (97%)
  local copies, waits for them, and re-layouts  0.71 us (2%)
    pallas_call x1, Pallas kernels, fused(): pl.pallas_call(functools.partial(fused_kernel, n, groups), out_shape=pltp...  31.2 us
    unnamed x1, local copies, waits for them, and re-layouts  0.71 us

profile of v3, /device:TPU:0, one launch (start us, length us, event | category | flops | bytes accessed | tf_op | source)
XLA Modules:
  0.0 31.9 jit_solution(6858259731554590611)
XLA Ops:
  0.0 31.2 %shard_map.73 = bf16[128,1024]{1,0:T(8,128)(2,1)S(1)} custom-call(bf16[128,1024]{1,0:T(8,128)(2,1)} %bitcast.8, bf16[128,512]{1,0:T(8,128)(2,1)} %bitcast.9, bf16[128,512]{1,0:T(8,128)(2,1)} %bitcast.10, bf16[64,128]{1,0:T(8,128)(2,1)} %bitcast.11, bf16[32,2048]{1,0:T(8,128)(2,1)} %codes_hbm.1, s32[4,16]{1,0:T(4,128)} %expo_ref.1, s32[1,256]{1,0:T(1,128)} %docs_ref.1), custom_call_target="tpu_custom_call" | custom-call | tf_op jit(solution)/shard_map/pallas_call | solution.py:384
  31.2 0.7 %copy.9 = bf16[1,128,1024]{2,1,0:T(8,128)(2,1)} copy(bf16[1,128,1024]{2,1,0:T(8,128)(2,1)S(1)} %bitcast.7) | data formatting | bytes 524288

commit v4 on v3

--- a/solution.py
+++ b/solution.py
@@ -75,7 +75,7 @@
 def fused_kernel(
     n, groups, qn_hbm, qr_hbm, lat_hbm, rope_hbm, codes_hbm, expo_ref, docs_ref,
     out_ref,
-    weight, lat_all, rope_all, qn, qr, attended, bias, peaks,
+    weight, lat_all, rope_all, qn, qr, attended, bias, partial, peaks,
     z_send, z_recv, y_send, y_recv, x_send, x_recv, c_send, c_recv,
     lat_send, lat_recv, local_sem, own_sem, peak_send, peak_recv, ready, entered,
 ):
@@ -261,10 +261,12 @@
         send_own(k, 0)
 
     z_stage(1, 0)
-    for k in from_source:
+    y_stage(0)
+    send_own(1, 1)
+    z_stage(2, 0)
+    for k in from_source[1:]:
         send_own(k, 1)
-    y_stage(0)
-    for k in range(2, planes):
+    for k in range(3, planes):
         z_stage(k, 0)
     y_stage(1)
     z_stage(1, 1)
@@ -283,20 +285,59 @@
     allowed = (keys_at <= places) & (jnp.broadcast_to(docs, (tok, length)) == mine)
     bias[...] = jnp.where(allowed, jnp.float32(0), jnp.float32(-1e30))
 
-    for k in range(2, planes):
+    wide = DN + DV
+    last = jnp.where(plane < planes // 2, planes - 1, 0)
+
+    def product(source, h):
+        block = pl.ds(pl.multiple_of(source * BLK, BLK), BLK)
+        line = []
+        for c in range(wide // BLK):
+            power = jnp.full((1, BLK), expo_ref[source, h * wide // BLK + c], jnp.int32)
+            factor = jnp.exp2(power.astype(jnp.float32)).astype(jnp.bfloat16)
+            line.append(
+                weight[block, h * wide + c * BLK : h * wide + (c + 1) * BLK] * factor
+            )
+        return jnp.dot(
+            lat_all[:, block], jnp.concatenate(line, axis=1), preferred_element_type=jnp.float32
+        )
+
+    def add_plane(k):
+        def body(d):
+            source = plane - steps[d] * k
+            for which in range(4):
+                core_in(k, d, which).wait_recv()
+
+            def add():
+                for h in range(heads):
+                    columns = slice(h * wide, (h + 1) * wide)
+                    if k == 0:
+                        partial[:, columns] = product(source, h)
+                    else:
+                        partial[:, columns] += product(source, h)
+
+            if k == 0:
+                add()
+            else:
+                pl.when(source != last)(add)
+
+        each(k, body)
+
+    y_stage(2)
+    add_plane(0)
+    for k in range(3, planes):
         y_stage(k)
     x_stage(1)
     for k in range(2, planes):
         z_stage(k, 1)
+    x_stage(2)
+    add_plane(1)
+    for k in range(3, planes):
+        x_stage(k)
     for k in range(2, planes):
-        x_stage(k)
-    for which in range(4):
-        for k in range(planes):
-            each(k, lambda d: core_in(k, d, which).wait_recv())
+        add_plane(k)
 
     pl.semaphore_signal(ready, inc=1, device_id=to_ctx, device_id_type=MESH)
 
-    latents = lat_all[...]
     rope = rope_all[...]
     blank = jnp.zeros_like(rope)
     rope_of = (
@@ -305,20 +346,8 @@
     dims_t = (((1,), (1,)), ((), ()))
     peak = jnp.zeros((tok, DV), jnp.float32)
     for h in range(heads):
-        at_col = h * (DN + DV)
-        blocks = []
-        for b in range(weight.shape[0] // BLK):
-            line = []
-            for c in range((DN + DV) // BLK):
-                power = jnp.full((1, BLK), expo_ref[b, at_col // BLK + c], jnp.int32)
-                factor = jnp.exp2(power.astype(jnp.float32)).astype(jnp.bfloat16)
-                line.append(
-                    weight[b * BLK : (b + 1) * BLK, at_col + c * BLK : at_col + (c + 1) * BLK]
-                    * factor
-                )
-            blocks.append(jnp.concatenate(line, axis=1))
-        scaled = jnp.concatenate(blocks, axis=0)
-        kv = jnp.dot(latents, scaled, preferred_element_type=jnp.float32).astype(jnp.bfloat16)
+        columns = slice(h * wide, (h + 1) * wide)
+        kv = (partial[:, columns] + product(last, h)).astype(jnp.bfloat16)
         pair = (h // 2) * 2 * DR
         queries = jnp.concatenate(
             [qn[:, h * DN : (h + 1) * DN], qr[:, pair : pair + 2 * DR]], axis=1
@@ -394,6 +423,7 @@
             pltpu.VMEM(q_rope.shape[1:], jnp.bfloat16),
             pltpu.VMEM((tok, width // 2), jnp.float32),
             pltpu.VMEM((tok, tok * groups), jnp.float32),
+            pltpu.VMEM((tok * groups, width), jnp.float32),
             pltpu.VMEM((n * groups, 1, LANES), jnp.float32),
             dma((planes, 2, 2)), dma((planes, 2, 2)),
             dma((planes, 2)), dma((planes, 2)), dma((planes, 2)), dma((planes, 2)),
@@ -421,7 +451,7 @@
 
     def body(*args):
         rows = args[4].shape[0]
-        if groups == 2 and n % 4 == 0 and rows % 32 == 0:
+        if groups == 2 and n % 4 == 0 and rows % 32 == 0 and rows * 4 == BLK and n >= 8:
             return fused(n, groups, *args)
         return per_device(*args)
 

time: 32.1 us -> 29.1 us (0.907)
  Pallas kernels: 31.2 us -> 28.3 us
    pallas_call x1, Pallas kernels: 31.2 us -> 28.3 us  [fused(): pl.pallas_call(functools.partial(fused_kernel, n, groups), out_shape=pltp...]
where the time goes in v4:
time: 29.1 us; the launch traced here: 29 us
  Pallas kernels  28.3 us (97%)
  local copies, waits for them, and re-layouts  0.71 us (2%)
    pallas_call x1, Pallas kernels, fused(): pl.pallas_call(functools.partial(fused_kernel, n, groups), out_shape=pltp...  28.3 us
    unnamed x1, local copies, waits for them, and re-layouts  0.71 us

profile of v4, /device:TPU:0, one launch (start us, length us, event | category | flops | bytes accessed | tf_op | source)
XLA Modules:
  0.0 29.0 jit_solution(5607196102266796823)
XLA Ops:
  0.0 28.3 %shard_map.73 = bf16[128,1024]{1,0:T(8,128)(2,1)S(1)} custom-call(bf16[128,1024]{1,0:T(8,128)(2,1)} %bitcast.8, bf16[128,512]{1,0:T(8,128)(2,1)} %bitcast.9, bf16[128,512]{1,0:T(8,128)(2,1)} %bitcast.10, bf16[64,128]{1,0:T(8,128)(2,1)} %bitcast.11, bf16[32,2048]{1,0:T(8,128)(2,1)} %codes_hbm.1, s32[4,16]{1,0:T(4,128)} %expo_ref.1, s32[1,256]{1,0:T(1,128)} %docs_ref.1), custom_call_target="tpu_custom_call" | custom-call | tf_op jit(solution)/shard_map/pallas_call | solution.py:413
  28.3 0.7 %copy.9 = bf16[1,128,1024]{2,1,0:T(8,128)(2,1)} copy(bf16[1,128,1024]{2,1,0:T(8,128)(2,1)S(1)} %bitcast.7) | data formatting | bytes 524288

commit v5 on v4

--- a/solution.py
+++ b/solution.py
@@ -73,9 +73,9 @@
 
 
 def fused_kernel(
-    n, groups, qn_hbm, qr_hbm, lat_hbm, rope_hbm, codes_hbm, expo_ref, docs_ref,
+    n, groups, qn_hbm, qr_hbm, lat_hbm, rope_hbm, codes_hbm, expo_hbm, docs_hbm,
     out_ref,
-    weight, lat_all, rope_all, qn, qr, attended, bias, partial, peaks,
+    weight, lat_all, rope_all, qn, qr, attended, bias, partial, rope_of, peaks, expo_ref, docs_ref,
     z_send, z_recv, y_send, y_recv, x_send, x_recv, c_send, c_recv,
     lat_send, lat_recv, local_sem, own_sem, peak_send, peak_recv, ready, entered,
 ):
@@ -105,6 +105,8 @@
         pltpu.make_async_copy(rope_hbm, rope_all.at[:, own], local_sem.at[1]),
         pltpu.make_async_copy(qn_hbm, qn, local_sem.at[2]),
         pltpu.make_async_copy(qr_hbm, qr, local_sem.at[3]),
+        pltpu.make_async_copy(expo_hbm, expo_ref, local_sem.at[4]),
+        pltpu.make_async_copy(docs_hbm, docs_ref, local_sem.at[5]),
         pltpu.make_async_copy(
             codes_hbm, weight.at[pl.ds(pl.multiple_of(f * rows, rows), rows)], own_sem
         ),
@@ -266,10 +268,10 @@
     z_stage(2, 0)
     for k in from_source[1:]:
         send_own(k, 1)
+    z_stage(1, 1)
+    y_stage(1)
     for k in range(3, planes):
         z_stage(k, 0)
-    y_stage(1)
-    z_stage(1, 1)
     x_stage(0)
 
     for copy in locals_:
@@ -284,6 +286,10 @@
     keys_at = lax.broadcasted_iota(jnp.int32, (tok, length), 1)
     allowed = (keys_at <= places) & (jnp.broadcast_to(docs, (tok, length)) == mine)
     bias[...] = jnp.where(allowed, jnp.float32(0), jnp.float32(-1e30))
+    rope = rope_all[...]
+    blank = jnp.zeros_like(rope)
+    rope_of[0] = jnp.concatenate([rope, blank], axis=0).T
+    rope_of[1] = jnp.concatenate([blank, rope], axis=0).T
 
     wide = DN + DV
     last = jnp.where(plane < planes // 2, planes - 1, 0)
@@ -338,11 +344,6 @@
 
     pl.semaphore_signal(ready, inc=1, device_id=to_ctx, device_id_type=MESH)
 
-    rope = rope_all[...]
-    blank = jnp.zeros_like(rope)
-    rope_of = (
-        jnp.concatenate([rope, blank], axis=0).T, jnp.concatenate([blank, rope], axis=0).T
-    )
     dims_t = (((1,), (1,)), ((), ()))
     peak = jnp.zeros((tok, DV), jnp.float32)
     for h in range(heads):
@@ -413,7 +414,7 @@
     scaled_out = pl.pallas_call(
         functools.partial(fused_kernel, n, groups),
         out_shape=pltpu.VMEM((tok, width // 2), jnp.bfloat16),
-        in_specs=[hbm] * 5 + [pl.BlockSpec(memory_space=pltpu.SMEM), vmem],
+        in_specs=[hbm] * 7,
         out_specs=vmem,
         scratch_shapes=[
             pltpu.VMEM((rows * n, width), jnp.bfloat16),
@@ -424,11 +425,14 @@
             pltpu.VMEM((tok, width // 2), jnp.float32),
             pltpu.VMEM((tok, tok * groups), jnp.float32),
             pltpu.VMEM((tok * groups, width), jnp.float32),
+            pltpu.VMEM((2, tok * groups, 2 * DR), jnp.bfloat16),
             pltpu.VMEM((n * groups, 1, LANES), jnp.float32),
+            pltpu.SMEM(exponents.shape, jnp.int32),
+            pltpu.VMEM(doc_ids.shape, jnp.int32),
             dma((planes, 2, 2)), dma((planes, 2, 2)),
             dma((planes, 2)), dma((planes, 2)), dma((planes, 2)), dma((planes, 2)),
             dma((4, planes, 2)), dma((4, planes, 2)),
-            dma((2,)), dma((2,)), dma((4,)), dma, dma, dma,
+            dma((2,)), dma((2,)), dma((6,)), dma, dma, dma,
             pltpu.SemaphoreType.REGULAR, pltpu.SemaphoreType.REGULAR((planes, 2)),
         ],
         compiler_params=pltpu.CompilerParams(collective_id=0, has_side_effects=True),

time: 29.1 us -> 28.4 us (0.976)
  Pallas kernels: 28.3 us -> 27.5 us
    pallas_call x1, Pallas kernels: 28.3 us -> 27.5 us  [fused(): pl.pallas_call(functools.partial(fused_kernel, n, groups), out_shape=pltp...]
where the time goes in v5:
time: 28.4 us; the launch traced here: 28.3 us
  Pallas kernels  27.5 us (97%)
  local copies, waits for them, and re-layouts  0.71 us (2%)
    pallas_call x1, Pallas kernels, fused(): pl.pallas_call(functools.partial(fused_kernel, n, groups), out_shape=pltp...  27.5 us
    unnamed x1, local copies, waits for them, and re-layouts  0.71 us

profile of v5, /device:TPU:0, one launch (start us, length us, event | category | flops | bytes accessed | tf_op | source)
XLA Modules:
  0.0 28.3 jit_solution(13414060338664687608)
XLA Ops:
  0.0 27.5 %shard_map.73 = bf16[128,1024]{1,0:T(8,128)(2,1)S(1)} custom-call(bf16[128,1024]{1,0:T(8,128)(2,1)} %bitcast.8, bf16[128,512]{1,0:T(8,128)(2,1)} %bitcast.9, bf16[128,512]{1,0:T(8,128)(2,1)} %bitcast.10, bf16[64,128]{1,0:T(8,128)(2,1)} %bitcast.11, bf16[32,2048]{1,0:T(8,128)(2,1)} %codes_hbm.1, s32[4,16]{1,0:T(4,128)} %expo_hbm.1, s32[1,256]{1,0:T(1,128)} %docs_hbm.1), custom_call_target="tpu_custom_call" | custom-call | tf_op jit(solution)/shard_map/pallas_call | solution.py:414
  27.6 0.7 %copy.9 = bf16[1,128,1024]{2,1,0:T(8,128)(2,1)} copy(bf16[1,128,1024]{2,1,0:T(8,128)(2,1)S(1)} %bitcast.7) | data formatting | bytes 524288

commit v6 on v5

--- a/solution.py
+++ b/solution.py
@@ -361,7 +361,7 @@
         total = jnp.sum(expo, axis=-1, keepdims=True)
         out = jnp.dot(
             expo.astype(jnp.bfloat16), kv[:, DN:], preferred_element_type=jnp.float32
-        ) / total
+        ) * (1.0 / total)
         attended[:, h * DV : (h + 1) * DV] = out
         peak = jnp.maximum(peak, jnp.abs(out))
 
@@ -400,7 +400,7 @@
     arrived.wait_send()
     arrived.wait_recv()
     amax = jnp.max(jnp.max(peaks[...], axis=0), axis=-1, keepdims=True)
-    out_ref[...] = (attended[...] / amax).astype(out_ref.dtype)
+    out_ref[...] = (attended[...] * (1.0 / amax)).astype(out_ref.dtype)
 
 
 def fused(n, groups, q_nope, q_rope, kv_latent, key_rope, weight_codes, exponents, doc_ids):

time: 28.4 us -> 28.4 us (level)
  no operation moved by 1% of the time
where the time goes in v6:
time: 28.4 us; the launch traced here: 28.3 us
  Pallas kernels  27.5 us (97%)
  local copies, waits for them, and re-layouts  0.71 us (2%)
    pallas_call x1, Pallas kernels, fused(): pl.pallas_call(functools.partial(fused_kernel, n, groups), out_shape=pltp...  27.5 us
    unnamed x1, local copies, waits for them, and re-layouts  0.71 us

profile of v6, /device:TPU:0, one launch (start us, length us, event | category | flops | bytes accessed | tf_op | source)
XLA Modules:
  0.0 28.3 jit_solution(1211472030204608300)
XLA Ops:
  0.0 27.5 %shard_map.73 = bf16[128,1024]{1,0:T(8,128)(2,1)S(1)} custom-call(bf16[128,1024]{1,0:T(8,128)(2,1)} %bitcast.8, bf16[128,512]{1,0:T(8,128)(2,1)} %bitcast.9, bf16[128,512]{1,0:T(8,128)(2,1)} %bitcast.10, bf16[64,128]{1,0:T(8,128)(2,1)} %bitcast.11, bf16[32,2048]{1,0:T(8,128)(2,1)} %codes_hbm.1, s32[4,16]{1,0:T(4,128)} %expo_hbm.1, s32[1,256]{1,0:T(1,128)} %docs_hbm.1), custom_call_target="tpu_custom_call" | custom-call | tf_op jit(solution)/shard_map/pallas_call | solution.py:414
  27.6 0.7 %copy.9 = bf16[1,128,1024]{2,1,0:T(8,128)(2,1)} copy(bf16[1,128,1024]{2,1,0:T(8,128)(2,1)S(1)} %bitcast.7) | data formatting | bytes 524288
